TPU v7x, 256 devices: a whole 4x4x8 slice. The times are simulated.
256 devices in a mesh: enc: 16 (over z, core), vocab: 8 (over x, y_hi), grp: 2 (over y_lo).
Axes of the slice: x: 4, y: 4 (y_hi: 2, y_lo: 2; y = y_hi * 2 + y_lo), z: 8, core: 2. Of those that a mesh axis runs over, the one named last changes fastest.
Arguments:
- hidden: bfloat16 [12288, 1024], P('enc', ('vocab', 'grp')), may hold values from -6 to 6
- dense_weight: bfloat16 [1024, 1024], P('enc'), may hold values from -0.1875 to 0.1875
- head_weight: bfloat16 [1024, 126976], P('enc', ('vocab', 'grp')), may hold values from -0.1875 to 0.1875
- head_bias: float32 [126976], P(('vocab', 'grp')), may hold values from -4 to 4
- lengths: int32 [48], P('enc'), may hold values from 64 to 256, as said below
- queries: bfloat16 [128, 126976], P('enc', ('vocab', 'grp')), may hold values from -0.25 to 0.25283518
- positives: int32 [128], replicated, may hold values from 0 to 47
Outputs:
- batch_loss: float32 [], replicated
- query_grad: float32 [128, 126976], P('enc', ('vocab', 'grp'))
- passage_grad: float32 [48, 126976], P('enc', ('vocab', 'grp'))
Inputs may be any that keep to these rules, and one draw needn't show every extreme that they name: `lengths`: each 3 passages in a row hold, among their first two, one with 256 valid tokens and one with 64.
All inputs are finite; a program needn't handle non-finite values.
Results may differ from a plain program's by a relative error of at most 0.035.
Values may be sent and summed in bfloat16 or wider, within the bound.
A program may use at most 128 MiB of HBM per device.

v0:
```python
import jax
import jax.numpy as jnp
from jax import lax
from jax.sharding import PartitionSpec as P


def finish_norm(pre_act):
    activated = jax.nn.gelu(pre_act, approximate=False)
    center = jnp.mean(activated, axis=-1, keepdims=True)
    spread = jnp.mean(jnp.square(activated - center), axis=-1, keepdims=True)
    return ((activated - center) * lax.rsqrt(spread + 1e-05)).astype(jnp.bfloat16)


def project(in_rows, dense_weight):
    pre_act = jnp.dot(
        in_rows,
        lax.all_gather(dense_weight, "enc", axis=0, tiled=True),
        preferred_element_type=jnp.float32,
    )
    return finish_norm(pre_act)


def pool_reps(logits, token_counts, seq_len):
    passages = token_counts.shape[0]
    by_passage = logits.reshape(passages, seq_len, logits.shape[1])
    positions = lax.broadcasted_iota(jnp.int32, (passages, seq_len), 1)
    is_valid = positions < token_counts[:, None]
    masked = jnp.where(is_valid[:, :, None], by_passage, -jnp.inf)
    peak_val = jnp.max(masked, axis=1)
    return jnp.log1p(jnp.maximum(peak_val, 0.0)).astype(jnp.bfloat16)


def softmax_grads(scores, chosen):
    peak_val = jnp.max(scores, axis=1, keepdims=True)
    log_total = jnp.log(jnp.sum(jnp.exp(scores - peak_val), axis=1, keepdims=True)) + peak_val
    columns = lax.broadcasted_iota(jnp.int32, scores.shape, 1)
    is_positive = columns == chosen[:, None]
    picked_score = jnp.sum(jnp.where(is_positive, scores, 0.0), axis=1)
    batch_loss = jnp.sum(log_total[:, 0] - picked_score)
    score_grad = (jnp.exp(scores - log_total) - is_positive.astype(jnp.float32)).astype(
        jnp.bfloat16
    )
    return (batch_loss, score_grad)


def per_device(hidden, dense_weight, head_weight, head_bias, lengths, queries, positives):
    pass_dev = lengths.shape[0]
    seq_len = hidden.shape[0] // pass_dev
    enc_index = lax.axis_index("enc")
    features_all = lax.all_gather(hidden, ("vocab", "grp"), axis=1, tiled=True)
    normed = project(features_all, dense_weight)
    logits = jnp.dot(
        normed,
        lax.all_gather(head_weight, "enc", axis=0, tiled=True),
        preferred_element_type=jnp.float32,
    )
    pass_reps = pool_reps(logits + head_bias, lengths, seq_len)
    all_queries = lax.all_gather(queries, "enc", axis=0, tiled=True)
    partial_value = lax.dot_general(
        all_queries, pass_reps, (((1,), (1,)), ((), ())), preferred_element_type=jnp.float32
    )
    local_scores = lax.psum(partial_value, ("vocab", "grp"))
    scores = lax.all_gather(local_scores, "enc", axis=1, tiled=True)
    loss_sum, score_grad = softmax_grads(scores, positives)
    batch_loss = loss_sum / scores.shape[0]
    own_grad = lax.dynamic_slice_in_dim(score_grad, enc_index * pass_dev, pass_dev, 1)
    query_grad = lax.psum_scatter(
        jnp.dot(own_grad, pass_reps, preferred_element_type=jnp.float32),
        "enc",
        scatter_dimension=0,
        tiled=True,
    )
    passage_grad = lax.dot_general(
        own_grad, all_queries, (((0,), (0,)), ((), ())), preferred_element_type=jnp.float32
    )
    return (batch_loss, query_grad, passage_grad)


def solution(mesh):
    placed = (
        P("enc", ("vocab", "grp")),
        P("enc", None),
        P("enc", ("vocab", "grp")),
        P(("vocab", "grp")),
        P("enc"),
        P("enc", ("vocab", "grp")),
        P(),
    )
    return jax.shard_map(
        per_device,
        mesh=mesh,
        in_specs=placed,
        out_specs=(P(), P("enc", ("vocab", "grp")), P("enc", ("vocab", "grp"))),
        check_vma=False,
    )
```

profile of v0, /device:TPU:1, one launch (start us, length us, event | category | flops | bytes accessed | tf_op | source)
XLA Modules:
  0.0 360.9 jit_solution(3995243074012879067)
XLA Ops:
  7.2 0.0 all-gather.6.cloned.1.call-start
  7.2 0.7 all-gather.6.cloned.1.call-update
  7.9 0.0 all-gather.8.cloned.1.call-start
  7.9 0.7 all-gather.8.cloned.1.call-update
  8.6 0.0 all-gather.10.cloned.1.call-start
  8.7 0.7 all-gather.10.cloned.1.call-update
  9.4 0.0 all-gather.12.cloned.1.call-start
  9.4 0.5 all-gather.12.cloned.1.call-update
  10.0 0.0 reduce-scatter.2.cloned.1.call-start
  10.0 0.7 iota_compare_fusion.1
  10.7 0.7 iota_compare_fusion
  11.4 50.9 %all-gather.6.cloned.1.call-done = bf16[768,1024]{0,1:T(8,128)(2,1)} async-done(((bf16[768,64]{0,1:T(8,128)(2,1)}), bf16[768,1024]{0,1:T(8,128)(2,1)}) %all-gather.6.cloned.1.call-update) | async-done | bytes 1572880 | tf_op jit(solution)/shard_map/all_gather | solution.py:50
  62.3 42.4 %all-gather.8.cloned.1.call-done = bf16[1024,1024]{1,0:T(8,128)(2,1)} async-done(((bf16[64,1024]{1,0:T(8,128)(2,1)}), bf16[1024,1024]{1,0:T(8,128)(2,1)}) %all-gather.8.cloned.1.call-update) | async-done | bytes 2097168 | tf_op jit(solution)/shard_map/all_gather | solution.py:17
  104.7 10.5 %fusion.17 = (f32[768]{0:T(1024)S(1)}, f32[768,1024]{1,0:T(8,128)S(1)}) fusion(bf16[768,1024]{0,1:T(8,128)(2,1)} %all-gather.6.cloned.1.call-done, bf16[1024,1024]{1,0:T(8,128)(2,1)} %all-gather.8.cloned.1.call-done), kind=kOutput, calls=%fused_computation.41 | convolution fusion | flops 1661730048 | bytes 6818816 | tf_op jit(solution)/shard_map/dot_general | solution.py:15
  115.2 0.0 copy-start.2
  115.3 0.4 multiply_reduce_fusion
  115.7 82.1 %all-gather.10.cloned.1.call-done = bf16[1024,7936]{1,0:T(8,128)(2,1)} async-done(((bf16[64,7936]{1,0:T(8,128)(2,1)}), bf16[1024,7936]{1,0:T(8,128)(2,1)}) %all-gather.10.cloned.1.call-update) | async-done | bytes 16252944 | tf_op jit(solution)/shard_map/all_gather | solution.py:54
  197.8 0.0 copy-done.2
  197.8 21.4 %convolution_add_fusion = f32[768,7936]{1,0:T(8,128)} fusion(bf16[1024,7936]{1,0:T(8,128)(2,1)} %all-gather.10.cloned.1.call-done, f32[7936]{0:T(1024)S(1)} %copy-done.2, f32[768,1024]{1,0:T(8,128)S(1)} %get-tuple-element.8, f32[768]{0:T(1024)S(1)} %add_rsqrt_fusion, f32[768]{0:T(1024)S(1)} %broadcast_multiply_fusion), kind=kOutput, calls=%fused_computation.1 | convolution fusion | flops 12490702848 | bytes 43815936 | tf_op jit(solution)/shard_map/dot_general | solution.py:52
  219.2 0.0 copy-start.1
  219.2 9.5 %select_reduce_fusion = f32[3,7936]{1,0:T(4,128)S(1)} fusion(f32[3,256,7936]{2,1,0:T(8,128)} %bitcast.14, pred[3,256]{1,0:T(4,128)(4,1)S(1)} %iota_compare_fusion.1), kind=kLoop, calls=%fused_computation | loop fusion | flops 12165888 | bytes 24475392 | tf_op jit(solution)/shard_map/reduce_max | solution.py:29
  228.7 9.1 %all-gather.12.cloned.1.call-done = bf16[128,7936]{1,0:T(8,128)(2,1)} async-done(((bf16[8,7936]{1,0:T(8,128)(2,1)}), bf16[128,7936]{1,0:T(8,128)(2,1)}) %all-gather.12.cloned.1.call-update) | async-done | bytes 2031632 | tf_op jit(solution)/shard_map/all_gather | solution.py:58
  237.8 2.2 convolution_bitcast_fusion
  240.0 33.3 %psum.7 = f32[128,3]{0,1:T(4,128)S(1)} all-reduce(f32[128,3]{0,1:T(4,128)S(1)} %convolution_bitcast_fusion), channel_id=1, replica_groups=mesh['enc'=16,'vocab'=8,'grp'=2] {'vocab','grp'}, use_global_device_ids=true, to_apply=%region_3.4 | all-reduce | flops 384 | bytes 3072 | tf_op jit(solution)/shard_map/psum | solution.py:62
  273.2 22.8 %all-gather = f32[16,3,128]{2,1,0:T(4,128)S(1)} all-gather(f32[1,3,128]{2,1,0:T(4,128)S(1)} %bitcast.17), channel_id=1, replica_groups=mesh['enc'=16,'vocab'=8,'grp'=2] {'enc'}, dimensions={0}, use_global_device_ids=true | all-gather | bytes 26112 | tf_op jit(solution)/shard_map/all_gather | solution.py:63
  296.1 0.0 copy-done.1
  296.2 0.6 subtract_reduce_fusion
  296.8 0.0 copy-start
  296.8 2.7 fusion.14
  299.4 0.0 reduce-scatter.2.cloned.1.call-update
  300.1 0.0 copy-done
  300.1 1.0 fusion.20
  301.1 52.1 %reduce-scatter.2.cloned.1.call-done = f32[8,7936]{1,0:T(8,128)} async-done(((f32[128,7936]{1,0:T(8,128)}), f32[8,7936]{1,0:T(8,128)}) %reduce-scatter.2.cloned.1.call-update) | async-done | bytes 253968 | tf_op jit(solution)/shard_map/reduce_scatter | solution.py:67
  (5 shorter events, 0.1 us)
Async XLA Ops:
  7.2 55.2 %all-gather.6.cloned.1.call-start = ((), (), s32[]{:S(2)}) async-start(), calls=%async_computation.1 | async-start | bytes 1671168 | tf_op jit(solution)/shard_map/all_gather | solution.py:50
  7.9 96.8 %all-gather.8.cloned.1.call-start = ((), (), s32[]{:S(2)}) async-start(), calls=%async_computation.2 | async-start | bytes 2228224 | tf_op jit(solution)/shard_map/all_gather | solution.py:17
  8.6 189.2 %all-gather.10.cloned.1.call-start = ((), (), s32[]{:S(2)}) async-start(), calls=%async_computation.3 | async-start | bytes 17268736 | tf_op jit(solution)/shard_map/all_gather | solution.py:54
  9.4 228.4 %all-gather.12.cloned.1.call-start = ((), (), s32[]{:S(2)}) async-start(), calls=%async_computation.4 | async-start | bytes 2158592 | tf_op jit(solution)/shard_map/all_gather | solution.py:58
  10.0 343.2 %reduce-scatter.2.cloned.1.call-start = ((), (), s32[]{:S(2)}) async-start(), calls=%async_computation.5 | async-start | bytes 4317184 | tf_op jit(solution)/shard_map/reduce_scatter | solution.py:67
  115.2 82.6 %copy-start.2 = (f32[7936]{0:T(1024)S(1)}, f32[7936]{0:T(1024)}, u32[]{:S(2)}) copy-start(f32[7936]{0:T(1024)} %param.10) | copy-start | bytes 95236
  219.2 76.9 %copy-start.1 = (s32[128]{0:T(128)S(1)}, s32[128]{0:T(128)}, u32[]{:S(2)}) copy-start(s32[128]{0:T(128)} %param.13) | copy-start | bytes 1540
  296.8 3.3 copy-start
Sparse Core Ops, SparseCore 0:
  10.5 51.7 all-gather.5
  64.1 40.5 all-gather.7
  106.5 91.2 all-gather.9
  199.5 38.2 all-gather.11
  299.6 53.5 reduce-scatter.1
where the time goes:
time: 363 us; the launch traced here: 361 us
  waiting for transfers between devices  239 us (66%)
  blocking collectives  56.1 us (15%)
  matrix products  37.8 us (10%)
  between operations  15.6 us (4%)
  other arithmetic  12 us (3%)
    all_gather x1, waiting for transfers between devices, per_device(): lax.all_gather(head_weight, 'enc', axis=0, tiled=True)  82.1 us
    reduce_scatter x1, waiting for transfers between devices, per_device(): lax.psum_scatter(jnp.dot(own_grad, pass_reps, preferred_element_type=jnp....  52.1 us
    all_gather x1, waiting for transfers between devices, per_device(): features_all = lax.all_gather(hidden, ('vocab', 'grp'), axis=1, tiled=True)  50.9 us
    all_gather x1, waiting for transfers between devices, project(): lax.all_gather(dense_weight, 'enc', axis=0, tiled=True)  42.4 us
    psum x1, blocking collectives, per_device(): local_scores = lax.psum(partial_value, ('vocab', 'grp'))  33.3 us
    all_gather x1, blocking collectives, per_device(): scores = lax.all_gather(local_scores, 'enc', axis=1, tiled=True)  22.8 us
    dot_general x1, matrix products, per_device(): jnp.dot(normed, lax.all_gather(head_weight, 'enc', axis=0, tiled=True), p...  21.4 us
    dot_general x1, matrix products, project(): jnp.dot(in_rows, lax.all_gather(dense_weight, 'enc', axis=0, tiled=True),...  10.5 us
  transfers between devices with their start and end apart: 5, of which 5 were waited for; matrix products, arithmetic and copies ran while one was open for 12% of the time, Pallas kernels for 0%

commit v1 on v0

v1 whole, which is shorter than its diff:
```python
import jax
import jax.numpy as jnp
import numpy as np
from jax import lax
from jax.experimental import pallas as pl
from jax.experimental.pallas import tpu as pltpu
from jax.sharding import PartitionSpec as P

NX, NY, NZ = 4, 4, 8
NE, NV = 16, 16
D = 1024
FW = D // NY
COLS = 7936
CW = 512
BIG, SHORT = 128, 32
ROWS = BIG + SHORT
NQ = 128
REPS = 48
HALF = REPS // 2
MESH = pl.DeviceIdType.MESH
F32, BF16 = jnp.float32, jnp.bfloat16
AWAY = (1, 15, 2, 14, 3, 13, 4, 12, 5, 11, 6, 10, 7, 9, 8)


def place():
    enc, vocab, grp = lax.axis_index("enc"), lax.axis_index("vocab"), lax.axis_index("grp")
    return enc // 2, enc % 2, vocab // 2, (vocab % 2) * 2 + grp


def device(z, c, x, y):
    return (2 * z + c, 2 * x + y // 2, y % 2)


def first_col(enc):
    return pl.multiple_of(jnp.minimum(CW * enc, COLS - CW), 128)


def aligned(start, size):
    return pl.ds(pl.multiple_of(start, size), size)


def arrived(ref, sem):
    pltpu.make_async_copy(ref, ref, sem).wait()


def send(src, dst, send_sem, recv_sem, to):
    pltpu.make_async_remote_copy(
        src_ref=src, dst_ref=dst, send_sem=send_sem, recv_sem=recv_sem,
        device_id=to, device_id_type=MESH,
    ).start()


def ring_order(z):
    return [(z + off + NZ) % NZ for off in (0, -1, 1, -2, 2, -3, 3, -4)]


def kernel(
    lens, hid, dense, weight, queries, bias, positives, loss, query_out, pass_out,
    hidv, hsel, hrecv, xrows, dn, act, stat, stat_all, tb, wx, pool, mx, qall, qfull, rfull,
    biasv, sp, cbuf, xbuf, ybuf, zbuf, fin, gradT,
    loc, h_s, h_r, d_s, d_r, ds_s, w_s, w_r, q_s, q_r, st_s, st_r,
    tz_s, ty_s, t_r, ts_s, ts_r, wx_s, wx_r, g_s, g_r, gs_s, p_s, p_r,
    r_s, r_r, rs_s, c_s, c_r, x_s, x_r, y_s, y_r, z_s, z_r,
):
    z, c, x, y = place()
    enc, v = 2 * z + c, 4 * x + y
    zs = ring_order(z)
    up, down = device((z + 1) % NZ, c, x, y), device((z + NZ - 1) % NZ, c, x, y)
    sibling = device(z, 1 - c, x, y)
    xr, xl, xo = (x + 1) % NX, (x + 3) % NX, (x + 2) % NX
    yr, yl, yo = (y + 1) % NY, (y + 3) % NY, (y + 2) % NY
    features = aligned(FW * y, FW)

    def dense_rows(zz, cc):
        return dn.at[aligned(64 * (2 * zz + cc), 64), :]

    def w_rows(xx, ee):
        return wx.at[xx, aligned(64 * ee, 64), :]

    def w_pair(xx, zz):
        return wx.at[xx, aligned(128 * zz, 128), :]

    def q_part(ee):
        return qall.at[aligned(8 * ee, 8), :]

    def q_rows(zz, cc):
        return qfull.at[aligned(8 * (2 * zz + cc), 8), :]

    own_hid = pltpu.make_async_copy(hid, hidv, loc.at[0])
    own_hid.start()
    own_cols = pl.ds(first_col(enc), CW)
    own_dense = pltpu.make_async_copy(dense.at[:, features], dense_rows(z, c), loc.at[1])
    own_w = pltpu.make_async_copy(weight.at[:, own_cols], w_rows(x, enc), loc.at[2])
    own_q = pltpu.make_async_copy(queries.at[:, own_cols], q_part(enc), loc.at[3])
    own_rows = pltpu.make_async_copy(queries, q_rows(z, c), loc.at[4])
    own_bias = pltpu.make_async_copy(bias.at[:, own_cols], biasv, loc.at[5])
    for copy in (own_dense, own_w, own_q, own_rows, own_bias):
        copy.start()

    bar = pltpu.get_barrier_semaphore()
    for i in range(1, NE):
        to = (enc + i) % NE
        pl.semaphore_signal(
            bar, inc=1, device_id=device(to // 2, to % 2, x, y), device_id_type=MESH
        )
    for i in range(1, 2 * NV):
        if i != NV:
            at = (16 * c + v + i) % 32
            pl.semaphore_signal(
                bar, inc=1, device_id=device(z, at // 16, (at // 4) % 4, at % 4),
                device_id_type=MESH,
            )

    own_hid.wait()
    n_first, n_third = lens[0], lens[2]
    swapped = jnp.full((64, 256), n_first, jnp.int32) < 256
    first, second = hidv[:, 0:256].astype(F32), hidv[:, 256:512].astype(F32)
    third = hidv[:, 512:768].astype(F32)
    full = jnp.where(swapped, second, first).astype(BF16)
    part = jnp.where(swapped, first, second).astype(BF16)[:, 0:128]
    lane = lax.broadcasted_iota(jnp.int32, (64, 256), 1)
    third = jnp.where(lane < n_third, third, jnp.broadcast_to(third[:, 0:1], (64, 256))).astype(BF16)
    for half in range(2):
        hsel[half, :, 0:128] = full[:, 128 * half : 128 * half + 128]
        hsel[2 + half, :, 0:128] = third[:, 128 * half : 128 * half + 128]
        hsel[half, :, 128:256] = part
        hsel[2 + half, :, 128:256] = part

    pl.semaphore_wait(bar, 15 + 30)

    for i in range(1, NZ):
        send(dense.at[:, features], dense_rows(z, c), d_s.at[i - 1], d_r.at[enc],
             device((z + (1, 7, 2, 6, 3, 5, 4)[i - 1]) % NZ, c, x, y))
    send(dense.at[:, features], dense_rows(z, c), ds_s.at[z], d_r.at[enc], sibling)

    h_to = hrecv.at[aligned(64 * v, 64), :]

    def hidden_dest(i):
        j = (8 * (x % 2) + 2 * y + c + i) % 16
        return j // 8, (j // 2) % 4, j % 2

    for i in range(16):
        kind, yd, cd = hidden_dest(i)
        xd = 2 * c + kind
        src = hsel.at[2 * kind + cd]
        mine = jnp.logical_and(cd == c, jnp.logical_and(xd == x, yd == y))

        @pl.when(mine)
        def _():
            pltpu.make_async_copy(src, h_to, h_r.at[v]).start()

        @pl.when(jnp.logical_not(mine))
        def _():
            send(src, h_to, h_s.at[i], h_r.at[v], device(z, cd, xd, yd))

    for n, i in enumerate(AWAY):
        to = (enc + i) % NE
        send(weight.at[:, pl.ds(first_col(to), CW)], w_rows(x, enc), w_s.at[n], w_r.at[enc],
             device(to // 2, to % 2, x, y))
    for n, i in enumerate(AWAY):
        to = (enc + i) % NE
        send(queries.at[:, pl.ds(first_col(to), CW)], q_part(enc), q_s.at[n], q_r.at[enc],
             device(to // 2, to % 2, x, y))

    def weights_first(k):
        zz = zs[k]
        if k == 0:
            own_w.wait()
            arrived(w_rows(x, 2 * z + 1 - c), w_r.at[2 * z + 1 - c])
        else:
            arrived(w_rows(x, 2 * zz), w_r.at[2 * zz])
            arrived(w_rows(x, 2 * zz + 1), w_r.at[2 * zz + 1])
        pair, sem = w_pair(x, zz), wx_r.at[8 * x + zz]
        send(pair, pair, wx_s.at[3 * k], sem, device(z, c, xr, y))
        send(pair, pair, wx_s.at[3 * k + 1], sem, device(z, c, xl, y))

    def weights_second(k):
        zz = zs[k]
        arrived(w_pair(xl, zz), wx_r.at[8 * xl + zz])
        arrived(w_pair(xr, zz), wx_r.at[8 * xr + zz])
        origin, to = (xl, xr) if k % 2 == 0 else (xr, xl)
        pair = w_pair(origin, zz)
        send(pair, pair, wx_s.at[3 * k + 2], wx_r.at[8 * origin + zz], device(z, c, to, y))

    def rows_of(zz, yy):
        return tb.at[zz, aligned(ROWS * c, ROWS), aligned(FW * yy, FW)]

    def core_rows(zz, cc):
        return tb.at[zz, aligned(ROWS * cc, ROWS), :]

    def ring_sends(k, rows, sems, base, sem):
        if k == 0:
            send(rows, rows, sems.at[0], sem, up)
            send(rows, rows, sems.at[6], sem, down)
        elif k % 2 == 1 and k < 7:
            send(rows, rows, sems.at[k], sem, up)
        elif k % 2 == 0 and k < 6:
            send(rows, rows, sems.at[k], sem, down)

    def tokens_first(k):
        zz = zs[k]
        rows, sem = rows_of(zz, y), t_r.at[4 * zz + y]
        if k:
            arrived(rows, sem)
        ring_sends(k, rows, tz_s, 0, sem)
        send(rows, rows, ty_s.at[3 * k], sem, device(z, c, x, yr))
        send(rows, rows, ty_s.at[3 * k + 1], sem, device(z, c, x, yl))

    def tokens_second(k):
        zz = zs[k]
        arrived(rows_of(zz, yl), t_r.at[4 * zz + yl])
        arrived(rows_of(zz, yr), t_r.at[4 * zz + yr])
        origin, to = (yl, yr) if k % 2 == 0 else (yr, yl)
        rows = rows_of(zz, origin)
        send(rows, rows, ty_s.at[3 * k + 2], t_r.at[4 * zz + origin], device(z, c, x, to))

    def tokens_third(k):
        zz = zs[k]
        arrived(rows_of(zz, yo), t_r.at[4 * zz + yo])
        rows = core_rows(zz, c)
        send(rows, rows, ts_s.at[k], ts_r.at[zz], sibling)

    def queries_ring(k):
        zz = zs[k]
        rows, sem = q_rows(zz, c), g_r.at[2 * zz + c]
        if k:
            arrived(rows, sem)
        else:
            own_rows.wait()
        ring_sends(k, rows, g_s, 0, sem)
        send(rows, rows, gs_s.at[k], sem, sibling)

    def dense_gather():
        for k in range(1, NZ):
            rows, sem = dense_rows(zs[k], c), d_r.at[2 * zs[k] + c]
            arrived(rows, sem)
            send(rows, rows, ds_s.at[zs[k]], sem, sibling)
        own_dense.wait()
        for zz in range(NZ):
            arrived(dense_rows(zz, 1 - c), d_r.at[2 * zz + 1 - c])

    def dense_layer():
        for vv in range(NV):
            arrived(hrecv.at[pl.ds(64 * vv, 64), :], h_r.at[vv])
        xrows[...] = hrecv[...].astype(F32).T
        own = jnp.concatenate(
            [xrows[0:BIG, :], xrows[pl.ds(pl.multiple_of(BIG + SHORT * c, SHORT), SHORT), :]], axis=0
        ).astype(BF16)
        pre_act = jnp.dot(own, dn[...], preferred_element_type=F32)
        activated = 0.5 * pre_act * (1.0 + lax.erf(pre_act * np.float32(np.sqrt(0.5))))
        act[...] = activated
        center = jnp.mean(activated, axis=-1, keepdims=True)
        square = jnp.sum(jnp.square(activated - center), axis=-1, keepdims=True)
        lane = lax.broadcasted_iota(jnp.int32, (ROWS, 128), 1)
        stat[0:ROWS, :] = jnp.where(lane == 0, center, square)
        stat[ROWS:256, :] = jnp.zeros((256 - ROWS, 128), F32)
        stat_all[y] = stat[...].T[0:8, :]
        for i in range(1, NY):
            send(stat_all.at[y], stat_all.at[y], st_s.at[i - 1], st_r.at[y],
                 device(z, c, x, (y + i) % NY))

    def normalize():
        for i in range(1, NY):
            arrived(stat_all.at[(y + i) % NY], st_r.at[(y + i) % NY])
        centers, squares = stat_all[:, 0:1, :], stat_all[:, 1:2, :]
        center = jnp.mean(centers, axis=0)
        spread = jnp.sum(squares + FW * jnp.square(centers - center[None]), axis=0) * (1.0 / D)
        scale = lax.rsqrt(spread + 1e-05)
        row = lax.broadcasted_iota(jnp.int32, (128, 256), 0)
        both = jnp.where(
            row == 0, jnp.broadcast_to(center, (128, 256)), jnp.broadcast_to(scale, (128, 256))
        ).T
        normed = (act[...] - both[0:ROWS, 0:1]) * both[0:ROWS, 1:2]
        tb[z, aligned(ROWS * c, ROWS), features] = normed.astype(BF16)

    weights_first(0)
    dense_gather()
    weights_first(1)
    weights_first(2)
    dense_layer()
    weights_second(0)
    normalize()
    tokens_first(0)
    weights_first(3)
    weights_first(4)
    weights_second(1)
    tokens_first(1)
    tokens_first(2)
    tokens_second(0)
    weights_second(2)
    weights_first(5)
    weights_first(6)
    tokens_first(3)
    tokens_first(4)
    tokens_second(1)
    tokens_second(2)
    weights_first(7)
    weights_second(3)
    weights_second(4)
    tokens_first(5)
    tokens_first(6)
    tokens_first(7)
    for k in (3, 4, 5, 6, 7):
        tokens_second(k)
        tokens_third(k - 3)
        if k > 4:
            weights_second(k)
    queries_ring(0)
    for k in (5, 6, 7):
        tokens_third(k)
    for k in range(1, NZ):
        queries_ring(k)

    for zz in range(NZ):
        arrived(core_rows(zz, 1 - c), ts_r.at[zz])

    def over_columns(i, _):
        xx = (x + i + i // 2 - 2 * (i // 3)) % NX

        @pl.when(i == 3)
        def _():
            for zz in range(NZ):
                arrived(w_pair(xo, zz), wx_r.at[8 * xo + zz])

        def over_rows(h, _):
            logits = jnp.dot(
                tb[pl.ds(4 * h, 4)].reshape(8 * ROWS, D), wx[xx], preferred_element_type=F32
            ).reshape(8, ROWS, CW)
            for u in range(4):
                top = jnp.maximum(
                    jnp.max(logits[2 * u, 0:BIG], axis=0, keepdims=True),
                    jnp.max(logits[2 * u + 1, 0:BIG], axis=0, keepdims=True),
                )
                low = jnp.maximum(
                    jnp.max(logits[2 * u, BIG:ROWS], axis=0, keepdims=True),
                    jnp.max(logits[2 * u + 1, BIG:ROWS], axis=0, keepdims=True),
                )
                pool[xx, pl.ds(4 * h + u, 1), :] = top
                pool[xx, pl.ds(8 + 4 * h + u, 1), :] = low
            return 0

        lax.fori_loop(0, 2, over_rows, 0)
        return 0

    lax.fori_loop(0, NX, over_columns, 0)

    for i in range(1, NX):
        to = (x + i) % NX
        send(pool.at[to], mx.at[x], p_s.at[i - 1], p_r.at[x], device(z, c, to, y))
    mx[x] = pool[x]
    own_q.wait()
    own_bias.wait()
    for i in range(1, NE):
        fr = (enc + i) % NE
        arrived(q_part(fr), q_r.at[fr])
    for i in range(1, NX):
        fr = (x + i) % NX
        arrived(mx.at[fr], p_r.at[fr])
    peaks = jnp.concatenate(
        [mx[0, 0:8], mx[2, 0:8], mx[0, 8:16], mx[2, 8:16], mx[1, 0:8], mx[3, 0:8]], axis=0
    ) + biasv[...]
    reps = jnp.log1p(jnp.maximum(peaks, 0.0)).astype(BF16)
    rfull[enc] = reps

    def reps_ring(k):
        zz = zs[k]
        rows, sem = rfull.at[2 * zz + c], r_r.at[2 * zz + c]
        if k:
            arrived(rows, sem)
        ring_sends(k, rows, r_s, 0, sem)
        send(rows, rows, rs_s.at[k], sem, sibling)

    col = lax.broadcasted_iota(jnp.int32, (REPS, CW), 1)
    doubled = jnp.where(enc == NE - 1, NE * CW - COLS, 0)
    counted = jnp.where(col < doubled, 0.0, reps.astype(F32)).astype(BF16)
    sp[...] = lax.dot_general(
        counted, qall[...], (((1,), (1,)), ((), ())), preferred_element_type=F32
    )

    swapped = jnp.where(jnp.full((8, NQ), lens[0], jnp.int32) < 256, 1.0, 0.0)
    cbuf[0, 0:HALF, :] = sp[aligned(HALF * (1 - c), HALF), :]
    cbuf[0, HALF : HALF + 8, :] = swapped
    send(cbuf.at[0], cbuf.at[1], c_s.at[0], c_r.at[0], sibling)
    reps_ring(0)
    arrived(cbuf.at[1], c_r.at[0])
    xbuf[x] = sp[aligned(HALF * c, HALF), :] + cbuf[1, 0:HALF, :]
    theirs = cbuf[1, HALF : HALF + 8, :]
    for i in range(1, NX):
        send(xbuf.at[x], xbuf.at[x], x_s.at[i - 1], x_r.at[x], device(z, c, (x + i) % NX, y))
    reps_ring(1)
    reps_ring(2)
    for i in range(1, NX):
        arrived(xbuf.at[(x + i) % NX], x_r.at[(x + i) % NX])
    ybuf[y] = (xbuf[0] + xbuf[1]) + (xbuf[2] + xbuf[3])
    for i in range(1, NY):
        send(ybuf.at[y], ybuf.at[y], y_s.at[i - 1], y_r.at[y], device(z, c, x, (y + i) % NY))
    reps_ring(3)
    reps_ring(4)
    for i in range(1, NY):
        arrived(ybuf.at[(y + i) % NY], y_r.at[(y + i) % NY])
    row = lax.broadcasted_iota(jnp.int32, (8, NQ), 0)
    zbuf[z, 0:HALF, :] = (ybuf[0] + ybuf[1]) + (ybuf[2] + ybuf[3])
    zbuf[z, HALF : HALF + 8, :] = jnp.where((row // 4) == c, swapped, theirs)
    for i, away in enumerate((1, 7, 2, 6, 3, 5, 4)):
        send(zbuf.at[z], zbuf.at[z], z_s.at[i], z_r.at[z], device((z + away) % NZ, c, x, y))
    for k in (5, 6, 7):
        reps_ring(k)
    for i in range(1, NZ):
        arrived(zbuf.at[(z + i) % NZ], z_r.at[(z + i) % NZ])
    fin[aligned(HALF * c, HALF), :] = jnp.sum(zbuf[:, 0:HALF, :], axis=0)
    half = fin.at[aligned(HALF * c, HALF), :]
    send(half, half, c_s.at[1], c_r.at[1], sibling)
    flips = jnp.concatenate(
        [zbuf[zz, HALF + 4 * cc : HALF + 4 * cc + 1, :] for cc in range(2) for zz in range(NZ)],
        axis=0,
    )
    block = lax.broadcasted_iota(jnp.int32, (NE, NQ), 0)
    base = 3 * (2 * (block % 8) + block // 8)
    flip = jnp.where(flips > 0.5, 1, 0)
    passage = jnp.concatenate([base + flip, base + 1 - flip, base + 2], axis=0)
    is_positive = passage == positives[...]
    other = fin.at[aligned(HALF * (1 - c), HALF), :]
    arrived(other, c_r.at[1])

    scores = fin[...]
    peak = jnp.max(scores, axis=0, keepdims=True)
    log_total = jnp.log(jnp.sum(jnp.exp(scores - peak), axis=0, keepdims=True)) + peak
    picked = jnp.sum(jnp.where(is_positive, scores, 0.0), axis=0, keepdims=True)
    loss[...] = jnp.broadcast_to(
        jnp.sum(log_total - picked, axis=1, keepdims=True) * (1.0 / NQ), (8, NQ)
    )
    grad = jnp.exp(scores - log_total) - jnp.where(is_positive, 1.0, 0.0)
    sp[...] = grad
    gradT[...] = jnp.concatenate([grad, jnp.zeros((NQ - REPS, NQ), F32)], axis=0).T
    for_query = gradT[aligned(8 * enc, 8), 0:REPS].astype(BF16)
    block = 8 * c + z
    full_row, part_row = sp[pl.ds(block, 1), :], sp[pl.ds(16 + block, 1), :]
    last_row = sp[pl.ds(32 + block, 1), :]
    mine = swapped[0:1, :] > 0.5
    for_passage = jnp.concatenate(
        [
            jnp.where(mine, part_row, full_row),
            jnp.where(mine, full_row, part_row),
            last_row,
            jnp.zeros((5, NQ), F32),
        ],
        axis=0,
    ).astype(BF16)
    for zz in range(NZ):
        arrived(rfull.at[2 * zz + 1 - c], r_r.at[2 * zz + 1 - c])
        arrived(q_rows(zz, 1 - c), g_r.at[2 * zz + 1 - c])
    for ee in range(NE):
        skip = NE * CW - COLS if ee == NE - 1 else 0
        cols = slice(CW * ee, CW * (ee + 1) - skip)
        query_out[:, cols] = jnp.dot(for_query, rfull[ee], preferred_element_type=F32)[:, skip:]
        pass_out[:, cols] = jnp.dot(for_passage, qfull[:, cols], preferred_element_type=F32)[0:3]

    for i in range(NE - 1):
        arrived(w_rows(x, enc), w_s.at[i])
        arrived(q_part(enc), q_s.at[i])
    for i in range(16):
        kind, yd, cd = hidden_dest(i)
        mine = jnp.logical_and(cd == c, jnp.logical_and(2 * c + kind == x, yd == y))

        @pl.when(jnp.logical_not(mine))
        def _():
            arrived(hsel.at[0], h_s.at[i])

    for k in range(7):
        arrived(dense_rows(z, c), d_s.at[k])
        arrived(rows_of(z, y), tz_s.at[k])
        arrived(q_rows(z, c), g_s.at[k])
        arrived(rfull.at[enc], r_s.at[k])
        arrived(zbuf.at[z], z_s.at[k])
    for k in range(NZ):
        arrived(dense_rows(z, c), ds_s.at[k])
        arrived(core_rows(z, c), ts_s.at[k])
        arrived(q_rows(z, c), gs_s.at[k])
        arrived(rfull.at[enc], rs_s.at[k])
    for k in range(24):
        arrived(rows_of(z, y), ty_s.at[k])
        arrived(w_pair(x, z), wx_s.at[k])
    for k in range(3):
        arrived(stat_all.at[y], st_s.at[k])
        arrived(mx.at[x], p_s.at[k])
        arrived(xbuf.at[x], x_s.at[k])
        arrived(ybuf.at[y], y_s.at[k])
    arrived(cbuf.at[0], c_s.at[0])
    arrived(half, c_s.at[1])


def call(lens, hid, dense, weight, queries, bias, positives):
    def dma(*n):
        return [pltpu.SemaphoreType.DMA((k,)) for k in n]

    hbm = pl.BlockSpec(memory_space=pltpu.HBM)
    vm = pl.BlockSpec(memory_space=pltpu.VMEM)
    return pl.pallas_call(
        kernel,
        out_shape=(
            jax.ShapeDtypeStruct((8, NQ), F32),
            jax.ShapeDtypeStruct((8, COLS), F32),
            jax.ShapeDtypeStruct((3, COLS), F32),
        ),
        in_specs=[pl.BlockSpec(memory_space=pltpu.SMEM), hbm, hbm, hbm, hbm, hbm, vm],
        out_specs=(vm, vm, vm),
        scratch_shapes=[
            pltpu.VMEM((64, 768), BF16),
            pltpu.VMEM((4, 64, 256), BF16),
            pltpu.VMEM((D, 256), BF16),
            pltpu.VMEM((256, D), F32),
            pltpu.VMEM((D, FW), BF16),
            pltpu.VMEM((ROWS, FW), F32),
            pltpu.VMEM((256, 128), F32),
            pltpu.VMEM((NY, 8, 256), F32),
            pltpu.VMEM((NZ, 2 * ROWS, D), BF16),
            pltpu.VMEM((NX, D, CW), BF16),
            pltpu.VMEM((NX, 16, CW), F32),
            pltpu.VMEM((NX, 16, CW), F32),
            pltpu.VMEM((NQ, CW), BF16),
            pltpu.VMEM((NQ, COLS), BF16),
            pltpu.VMEM((NE, REPS, CW), BF16),
            pltpu.VMEM((1, CW), F32),
            pltpu.VMEM((REPS, NQ), F32),
            pltpu.VMEM((2, HALF + 8, NQ), F32),
            pltpu.VMEM((NX, HALF, NQ), F32),
            pltpu.VMEM((NY, HALF, NQ), F32),
            pltpu.VMEM((NZ, HALF + 8, NQ), F32),
            pltpu.VMEM((REPS, NQ), F32),
            pltpu.VMEM((NQ, NQ), F32),
        ]
        + dma(6, 16, 16, 7, 16, 8, 15, 16, 15, 16, 3, 4)
        + dma(7, 24, 32, 8, 8, 24, 32, 7, 16, 8, 3, 4)
        + dma(7, 16, 8, 2, 2, 3, 4, 3, 4, 7, 8),
        compiler_params=pltpu.CompilerParams(
            collective_id=0, has_side_effects=True, vmem_limit_bytes=48 << 20
        ),
        name="splade_head",
    )(lens, hid, dense, weight, queries, bias, positives)


def per_device(hidden, dense_weight, head_weight, head_bias, lengths, queries, positives):
    loss, query_grad, passage_grad = call(
        lengths, hidden.T, dense_weight, head_weight, queries,
        head_bias.reshape(1, COLS), positives.reshape(1, NQ),
    )
    return loss[0, 0], query_grad, passage_grad


def solution(mesh):
    placed = (
        P("enc", ("vocab", "grp")),
        P("enc", None),
        P("enc", ("vocab", "grp")),
        P(("vocab", "grp")),
        P("enc"),
        P("enc", ("vocab", "grp")),
        P(),
    )
    return jax.shard_map(
        per_device,
        mesh=mesh,
        in_specs=placed,
        out_specs=(P(), P("enc", ("vocab", "grp")), P("enc", ("vocab", "grp"))),
        check_vma=False,
    )
```

time: 363 us -> 129 us (0.36)
  waiting for transfers between devices: 239 us -> 0 us
  Pallas kernels: 0 us -> 121 us
  blocking collectives: 56.1 us -> 0 us
  matrix products: 37.8 us -> 0 us
  between operations: 15.6 us -> 0.69 us
  other arithmetic: 12 us -> 0 us
  local copies, waits for them, and re-layouts: 0.03 us -> 6.56 us
    all_gather x4 -> x0, waiting for transfers between devices: 185 us -> none  [the longest x1 82.1 us: per_device(): lax.all_gather(head_weight, 'enc', axis=0, tiled=True)]
    pallas_call x0 -> x1, Pallas kernels: none -> 121 us  [call(): pl.pallas_call(kernel, out_shape=(jax.ShapeDtypeStruct((8, NQ), F32), jax...]
    reduce_scatter x1 -> x0, waiting for transfers between devices: 52.1 us -> none  [per_device(): lax.psum_scatter(jnp.dot(own_grad, pass_reps, preferred_element_type=jnp....]
    dot_general x5 -> x0, matrix products: 37.8 us -> none  [the longest x1 21.4 us: per_device(): jnp.dot(normed, lax.all_gather(head_weight, 'enc', axis=0, tiled=True), p...]
    psum x1 -> x0, blocking collectives: 33.3 us -> none  [per_device(): local_scores = lax.psum(partial_value, ('vocab', 'grp'))]
    all_gather x1 -> x0, blocking collectives: 22.8 us -> none  [per_device(): scores = lax.all_gather(local_scores, 'enc', axis=1, tiled=True)]
    reduce_max x2 -> x0, other arithmetic: 9.51 us -> none  [the longest x1 9.48 us: pool_reps(): peak_val = jnp.max(masked, axis=1)]
    unnamed x7 -> x14, local copies, waits for them, and re-layouts: 0.03 us -> 5.26 us
  transfers between devices with their start and end apart: 5 -> 0, of which waited for: 5 -> 0; matrix products, arithmetic and copies ran while one was open for 12% -> 0% of each run, Pallas kernels for 0% -> 0%
where the time goes in v1:
time: 129 us
  Pallas kernels  121 us (94%)
  local copies, waits for them, and re-layouts  6.56 us (5%)
    pallas_call x1, Pallas kernels, call(): pl.pallas_call(kernel, out_shape=(jax.ShapeDtypeStruct((8, NQ), F32), jax...  121 us
    unnamed x14, local copies, waits for them, and re-layouts  5.26 us

profile of v1, /device:TPU:1, one launch (start us, length us, event | category | flops | bytes accessed | tf_op | source)
XLA Modules:
  0.0 128.6 jit_solution(17106692480365299838)
XLA Ops:
  0.6 0.0 copy-start.4
  0.6 0.0 copy-start.5
  0.7 0.8 reshape.12.bias
  1.4 0.0 copy-done.4
  1.5 0.0 copy-done.5
  1.5 0.0 copy-start
  1.5 1.2 copy-done
  2.7 0.0 copy-start.1
  2.7 0.9 copy-done.1
  3.6 0.0 copy-start.2
  3.6 0.9 copy-done.2
  4.5 0.0 copy-start.3
  4.5 0.9 copy-done.3
  5.4 121.4 %splade_head.1 = (f32[8,128]{1,0:T(8,128)S(1)}, f32[8,7936]{1,0:T(8,128)S(1)}, f32[3,7936]{1,0:T(4,128)S(1)}) custom-call(s32[3]{0:T(128)S(1)} %copy-done.4, bf16[64,768]{1,0:T(8,128)(2,1)S(1)} %bitcast.3, bf16[64,1024]{1,0:T(8,128)(2,1)S(1)} %copy-done.1, bf16[64,7936]{1,0:T(8,128)(2,1)S(1)} %copy-done, bf16[8,7936]{1,0:T(8,128)(2,1)S(1)} %copy-done.2, ...), custom_call_target="tpu_custom_call" | custom-call | tf_op jit(solution)/shard_map/splade_head/pallas_call | solution.py:498
  126.8 0.5 slice.3
  127.3 0.7 copy.12
  128.0 0.6 copy.13
Async XLA Ops:
  0.6 0.8 copy-start.4
  0.6 0.8 copy-start.5
  1.5 1.2 copy-start
  2.7 0.9 copy-start.1
  3.6 0.9 copy-start.2
  4.5 0.9 copy-start.3

commit v2 on v1

--- a/solution.py
+++ b/solution.py
@@ -12,14 +12,13 @@
 FW = D // NY
 COLS = 7936
 CW = 512
-BIG, SHORT = 128, 32
+BIG, SHORT = 128, 16
 ROWS = BIG + SHORT
 NQ = 128
 REPS = 48
 HALF = REPS // 2
 MESH = pl.DeviceIdType.MESH
 F32, BF16 = jnp.float32, jnp.bfloat16
-AWAY = (1, 15, 2, 14, 3, 13, 4, 12, 5, 11, 6, 10, 7, 9, 8)
 
 
 def place():
@@ -74,14 +73,14 @@
     def dense_rows(zz, cc):
         return dn.at[aligned(64 * (2 * zz + cc), 64), :]
 
+    def q_part(ee):
+        return qall.at[aligned(8 * ee, 8), :]
+
     def w_rows(xx, ee):
         return wx.at[xx, aligned(64 * ee, 64), :]
 
     def w_pair(xx, zz):
         return wx.at[xx, aligned(128 * zz, 128), :]
-
-    def q_part(ee):
-        return qall.at[aligned(8 * ee, 8), :]
 
     def q_rows(zz, cc):
         return qfull.at[aligned(8 * (2 * zz + cc), 8), :]
@@ -153,14 +152,19 @@
         def _():
             send(src, h_to, h_s.at[i], h_r.at[v], device(z, cd, xd, yd))
 
-    for n, i in enumerate(AWAY):
-        to = (enc + i) % NE
-        send(weight.at[:, pl.ds(first_col(to), CW)], w_rows(x, enc), w_s.at[n], w_r.at[enc],
-             device(to // 2, to % 2, x, y))
-    for n, i in enumerate(AWAY):
-        to = (enc + i) % NE
-        send(queries.at[:, pl.ds(first_col(to), CW)], q_part(enc), q_s.at[n], q_r.at[enc],
-             device(to // 2, to % 2, x, y))
+    def weights_out(far):
+        for zz in ((z + far) % NZ, (z + NZ - far) % NZ)[: 1 if far in (0, 4) else 2]:
+            for cc in (1 - c,) if far == 0 else (c, 1 - c):
+                to = 2 * zz + cc
+                send(weight.at[:, pl.ds(first_col(to), CW)], w_rows(x, enc), w_s.at[to],
+                     w_r.at[enc], device(zz, cc, x, y))
+
+
+    def queries_out():
+        for i in range(1, NE):
+            to = (enc + i) % NE
+            send(queries.at[:, pl.ds(first_col(to), CW)], q_part(enc), q_s.at[i], q_r.at[enc],
+                 device(to // 2, to % 2, x, y))
 
     def weights_first(k):
         zz = zs[k]
@@ -182,11 +186,11 @@
         pair = w_pair(origin, zz)
         send(pair, pair, wx_s.at[3 * k + 2], wx_r.at[8 * origin + zz], device(z, c, to, y))
 
-    def rows_of(zz, yy):
-        return tb.at[zz, aligned(ROWS * c, ROWS), aligned(FW * yy, FW)]
-
-    def core_rows(zz, cc):
-        return tb.at[zz, aligned(ROWS * cc, ROWS), :]
+    def rows_of(k, yy):
+        return tb.at[k, aligned(ROWS * c, ROWS), aligned(FW * yy, FW)]
+
+    def core_rows(k, cc):
+        return tb.at[k, aligned(ROWS * cc, ROWS), :]
 
     def ring_sends(k, rows, sems, base, sem):
         if k == 0:
@@ -198,27 +202,28 @@
             send(rows, rows, sems.at[k], sem, down)
 
     def tokens_first(k):
-        zz = zs[k]
-        rows, sem = rows_of(zz, y), t_r.at[4 * zz + y]
+        rows, sem = rows_of(k, y), t_r.at[4 * k + y]
         if k:
             arrived(rows, sem)
-        ring_sends(k, rows, tz_s, 0, sem)
+        if k == 0:
+            send(rows, rows_of(1, y), tz_s.at[0], t_r.at[4 + y], up)
+            send(rows, rows_of(2, y), tz_s.at[6], t_r.at[8 + y], down)
+        elif k < 6:
+            send(rows, rows_of(k + 2, y), tz_s.at[k], t_r.at[4 * (k + 2) + y], up if k % 2 else down)
         send(rows, rows, ty_s.at[3 * k], sem, device(z, c, x, yr))
         send(rows, rows, ty_s.at[3 * k + 1], sem, device(z, c, x, yl))
 
     def tokens_second(k):
-        zz = zs[k]
-        arrived(rows_of(zz, yl), t_r.at[4 * zz + yl])
-        arrived(rows_of(zz, yr), t_r.at[4 * zz + yr])
+        arrived(rows_of(k, yl), t_r.at[4 * k + yl])
+        arrived(rows_of(k, yr), t_r.at[4 * k + yr])
         origin, to = (yl, yr) if k % 2 == 0 else (yr, yl)
-        rows = rows_of(zz, origin)
-        send(rows, rows, ty_s.at[3 * k + 2], t_r.at[4 * zz + origin], device(z, c, x, to))
+        rows = rows_of(k, origin)
+        send(rows, rows, ty_s.at[3 * k + 2], t_r.at[4 * k + origin], device(z, c, x, to))
 
     def tokens_third(k):
-        zz = zs[k]
-        arrived(rows_of(zz, yo), t_r.at[4 * zz + yo])
-        rows = core_rows(zz, c)
-        send(rows, rows, ts_s.at[k], ts_r.at[zz], sibling)
+        arrived(rows_of(k, yo), t_r.at[4 * k + yo])
+        rows = core_rows(k, c)
+        send(rows, rows, ts_s.at[k], ts_r.at[k], sibling)
 
     def queries_ring(k):
         zz = zs[k]
@@ -235,17 +240,19 @@
             rows, sem = dense_rows(zs[k], c), d_r.at[2 * zs[k] + c]
             arrived(rows, sem)
             send(rows, rows, ds_s.at[zs[k]], sem, sibling)
+
+    def hidden_here():
+        for vv in range(NV):
+            arrived(hrecv.at[pl.ds(64 * vv, 64), :], h_r.at[vv])
+        xrows[...] = hrecv[...].astype(F32).T
+
+    def dense_layer():
+        own = jnp.concatenate(
+            [xrows[0:BIG, :], xrows[aligned(BIG + SHORT * (2 * (x % 2) + c), SHORT), :]], axis=0
+        ).astype(BF16)
         own_dense.wait()
         for zz in range(NZ):
             arrived(dense_rows(zz, 1 - c), d_r.at[2 * zz + 1 - c])
-
-    def dense_layer():
-        for vv in range(NV):
-            arrived(hrecv.at[pl.ds(64 * vv, 64), :], h_r.at[vv])
-        xrows[...] = hrecv[...].astype(F32).T
-        own = jnp.concatenate(
-            [xrows[0:BIG, :], xrows[pl.ds(pl.multiple_of(BIG + SHORT * c, SHORT), SHORT), :]], axis=0
-        ).astype(BF16)
         pre_act = jnp.dot(own, dn[...], preferred_element_type=F32)
         activated = 0.5 * pre_act * (1.0 + lax.erf(pre_act * np.float32(np.sqrt(0.5))))
         act[...] = activated
@@ -271,93 +278,127 @@
             row == 0, jnp.broadcast_to(center, (128, 256)), jnp.broadcast_to(scale, (128, 256))
         ).T
         normed = (act[...] - both[0:ROWS, 0:1]) * both[0:ROWS, 1:2]
-        tb[z, aligned(ROWS * c, ROWS), features] = normed.astype(BF16)
-
+        tb[0, aligned(ROWS * c, ROWS), features] = normed.astype(BF16)
+
+    def weights_here():
+        for zz in range(NZ):
+            arrived(w_pair(xo, zz), wx_r.at[8 * xo + zz])
+
+    def pool_rows(first, size, xx):
+        logits = jnp.dot(
+            tb[first : first + size].reshape(size * 2 * ROWS, D), wx[xx],
+            preferred_element_type=F32,
+        ).reshape(2 * size, ROWS, CW)
+        for u in range(size):
+            zz = zs[first + u]
+            pool[xx, pl.ds(zz, 1), :] = jnp.maximum(
+                jnp.max(logits[2 * u, 0:BIG], axis=0, keepdims=True),
+                jnp.max(logits[2 * u + 1, 0:BIG], axis=0, keepdims=True),
+            )
+            pool[xx, pl.ds(8 + zz, 1), :] = jnp.maximum(
+                jnp.max(logits[2 * u, BIG:ROWS], axis=0, keepdims=True),
+                jnp.max(logits[2 * u + 1, BIG:ROWS], axis=0, keepdims=True),
+            )
+
+    def pooled(n, size):
+        for k in range(size * n, size * n + size):
+            arrived(core_rows(k, 1 - c), ts_r.at[k])
+
+        def over_columns(i, _):
+            xx = (x + i + i // 2) % NX
+            pool_rows(size * n, size, xx)
+            if size * (n + 1) == NZ:
+
+                @pl.when(i > 0)
+                def _():
+                    send(pool.at[xx], mx.at[x], p_s.at[i - 1], p_r.at[x], device(z, c, xx, y))
+
+            return 0
+
+        lax.fori_loop(0, NX - 1, over_columns, 0)
+
+    def pooled_last():
+        for first in (0, 4):
+            pool_rows(first, 4, xo)
+        send(pool.at[xo], mx.at[x], p_s.at[2], p_r.at[x], device(z, c, xo, y))
+
+    weights_out(0)
+    weights_out(1)
+    weights_out(2)
     weights_first(0)
     dense_gather()
     weights_first(1)
     weights_first(2)
+    weights_out(3)
+    hidden_here()
     dense_layer()
-    weights_second(0)
+    weights_first(3)
+    weights_first(4)
+    weights_out(4)
     normalize()
     tokens_first(0)
-    weights_first(3)
-    weights_first(4)
-    weights_second(1)
+    weights_first(5)
+    weights_first(6)
     tokens_first(1)
     tokens_first(2)
     tokens_second(0)
-    weights_second(2)
-    weights_first(5)
-    weights_first(6)
+    weights_second(0)
+    weights_second(1)
+    weights_first(7)
     tokens_first(3)
     tokens_first(4)
     tokens_second(1)
     tokens_second(2)
-    weights_first(7)
+    weights_second(2)
     weights_second(3)
-    weights_second(4)
     tokens_first(5)
     tokens_first(6)
+    tokens_third(0)
+    tokens_second(3)
+    tokens_third(1)
+    weights_second(4)
+    tokens_second(4)
+    tokens_third(2)
     tokens_first(7)
-    for k in (3, 4, 5, 6, 7):
-        tokens_second(k)
-        tokens_third(k - 3)
-        if k > 4:
-            weights_second(k)
+    weights_second(5)
+    tokens_second(5)
+    tokens_third(3)
+    weights_second(6)
+    tokens_second(6)
+    tokens_third(4)
+    weights_second(7)
+    queries_out()
     queries_ring(0)
-    for k in (5, 6, 7):
-        tokens_third(k)
-    for k in range(1, NZ):
-        queries_ring(k)
-
-    for zz in range(NZ):
-        arrived(core_rows(zz, 1 - c), ts_r.at[zz])
-
-    def over_columns(i, _):
-        xx = (x + i + i // 2 - 2 * (i // 3)) % NX
-
-        @pl.when(i == 3)
-        def _():
-            for zz in range(NZ):
-                arrived(w_pair(xo, zz), wx_r.at[8 * xo + zz])
-
-        def over_rows(h, _):
-            logits = jnp.dot(
-                tb[pl.ds(4 * h, 4)].reshape(8 * ROWS, D), wx[xx], preferred_element_type=F32
-            ).reshape(8, ROWS, CW)
-            for u in range(4):
-                top = jnp.maximum(
-                    jnp.max(logits[2 * u, 0:BIG], axis=0, keepdims=True),
-                    jnp.max(logits[2 * u + 1, 0:BIG], axis=0, keepdims=True),
-                )
-                low = jnp.maximum(
-                    jnp.max(logits[2 * u, BIG:ROWS], axis=0, keepdims=True),
-                    jnp.max(logits[2 * u + 1, BIG:ROWS], axis=0, keepdims=True),
-                )
-                pool[xx, pl.ds(4 * h + u, 1), :] = top
-                pool[xx, pl.ds(8 + 4 * h + u, 1), :] = low
-            return 0
-
-        lax.fori_loop(0, 2, over_rows, 0)
-        return 0
-
-    lax.fori_loop(0, NX, over_columns, 0)
-
-    for i in range(1, NX):
-        to = (x + i) % NX
-        send(pool.at[to], mx.at[x], p_s.at[i - 1], p_r.at[x], device(z, c, to, y))
+    pooled(0, 2)
+    tokens_second(7)
+    tokens_third(5)
+    pooled(1, 2)
+    tokens_third(6)
+    tokens_third(7)
+    queries_ring(1)
+    queries_ring(2)
+    pooled(2, 2)
+    pooled(3, 2)
+    queries_ring(3)
+    queries_ring(4)
+    weights_here()
+    pooled_last()
+
     mx[x] = pool[x]
-    own_q.wait()
     own_bias.wait()
-    for i in range(1, NE):
-        fr = (enc + i) % NE
-        arrived(q_part(fr), q_r.at[fr])
     for i in range(1, NX):
         fr = (x + i) % NX
         arrived(mx.at[fr], p_r.at[fr])
     peaks = jnp.concatenate(
-        [mx[0, 0:8], mx[2, 0:8], mx[0, 8:16], mx[2, 8:16], mx[1, 0:8], mx[3, 0:8]], axis=0
+        [
+            mx[0, 0:8],
+            mx[2, 0:8],
+            jnp.maximum(mx[0, 8:16], mx[1, 8:16]),
+            jnp.maximum(mx[2, 8:16], mx[3, 8:16]),
+            mx[1, 0:8],
+            mx[3, 0:8],
+        ],
+        axis=0,
     ) + biasv[...]
     reps = jnp.log1p(jnp.maximum(peaks, 0.0)).astype(BF16)
     rfull[enc] = reps
@@ -373,6 +414,9 @@
     col = lax.broadcasted_iota(jnp.int32, (REPS, CW), 1)
     doubled = jnp.where(enc == NE - 1, NE * CW - COLS, 0)
     counted = jnp.where(col < doubled, 0.0, reps.astype(F32)).astype(BF16)
+    own_q.wait()
+    for i in range(1, NE):
+        arrived(q_part((enc + i) % NE), q_r.at[(enc + i) % NE])
     sp[...] = lax.dot_general(
         counted, qall[...], (((1,), (1,)), ((), ())), preferred_element_type=F32
     )
@@ -382,6 +426,8 @@
     cbuf[0, HALF : HALF + 8, :] = swapped
     send(cbuf.at[0], cbuf.at[1], c_s.at[0], c_r.at[0], sibling)
     reps_ring(0)
+    queries_ring(5)
+    queries_ring(6)
     arrived(cbuf.at[1], c_r.at[0])
     xbuf[x] = sp[aligned(HALF * c, HALF), :] + cbuf[1, 0:HALF, :]
     theirs = cbuf[1, HALF : HALF + 8, :]
@@ -389,6 +435,7 @@
         send(xbuf.at[x], xbuf.at[x], x_s.at[i - 1], x_r.at[x], device(z, c, (x + i) % NX, y))
     reps_ring(1)
     reps_ring(2)
+    queries_ring(7)
     for i in range(1, NX):
         arrived(xbuf.at[(x + i) % NX], x_r.at[(x + i) % NX])
     ybuf[y] = (xbuf[0] + xbuf[1]) + (xbuf[2] + xbuf[3])
@@ -455,8 +502,8 @@
         query_out[:, cols] = jnp.dot(for_query, rfull[ee], preferred_element_type=F32)[:, skip:]
         pass_out[:, cols] = jnp.dot(for_passage, qfull[:, cols], preferred_element_type=F32)[0:3]
 
-    for i in range(NE - 1):
-        arrived(w_rows(x, enc), w_s.at[i])
+    for i in range(1, NE):
+        arrived(w_rows(x, enc), w_s.at[(enc + i) % NE])
         arrived(q_part(enc), q_s.at[i])
     for i in range(16):
         kind, yd, cd = hidden_dest(i)
@@ -468,17 +515,17 @@
 
     for k in range(7):
         arrived(dense_rows(z, c), d_s.at[k])
-        arrived(rows_of(z, y), tz_s.at[k])
+        arrived(rows_of(0, y), tz_s.at[k])
         arrived(q_rows(z, c), g_s.at[k])
         arrived(rfull.at[enc], r_s.at[k])
         arrived(zbuf.at[z], z_s.at[k])
     for k in range(NZ):
         arrived(dense_rows(z, c), ds_s.at[k])
-        arrived(core_rows(z, c), ts_s.at[k])
+        arrived(core_rows(0, c), ts_s.at[k])
         arrived(q_rows(z, c), gs_s.at[k])
         arrived(rfull.at[enc], rs_s.at[k])
     for k in range(24):
-        arrived(rows_of(z, y), ty_s.at[k])
+        arrived(rows_of(0, y), ty_s.at[k])
         arrived(w_pair(x, z), wx_s.at[k])
     for k in range(3):
         arrived(stat_all.at[y], st_s.at[k])
@@ -529,7 +576,7 @@
             pltpu.VMEM((REPS, NQ), F32),
             pltpu.VMEM((NQ, NQ), F32),
         ]
-        + dma(6, 16, 16, 7, 16, 8, 15, 16, 15, 16, 3, 4)
+        + dma(6, 16, 16, 7, 16, 8, 16, 16, 16, 16, 3, 4)
         + dma(7, 24, 32, 8, 8, 24, 32, 7, 16, 8, 3, 4)
         + dma(7, 16, 8, 2, 2, 3, 4, 3, 4, 7, 8),
         compiler_params=pltpu.CompilerParams(

time: 129 us -> 107 us (0.83)
  Pallas kernels: 121 us -> 99.4 us
    pallas_call x1, Pallas kernels: 121 us -> 99.4 us  [call(): pl.pallas_call(kernel, out_shape=(jax.ShapeDtypeStruct((8, NQ), F32), jax...]
where the time goes in v2:
time: 107 us
  Pallas kernels  99.4 us (93%)
  local copies, waits for them, and re-layouts  6.56 us (6%)
    pallas_call x1, Pallas kernels, call(): pl.pallas_call(kernel, out_shape=(jax.ShapeDtypeStruct((8, NQ), F32), jax...  99.4 us
    unnamed x14, local copies, waits for them, and re-layouts  5.26 us

profile of v2, /device:TPU:1, one launch (start us, length us, event | category | flops | bytes accessed | tf_op | source)
XLA Modules:
  0.0 106.7 jit_solution(13544028357789426545)
XLA Ops:
  0.6 0.0 copy-start.4
  0.6 0.0 copy-start.5
  0.7 0.8 reshape.12.bias
  1.4 0.0 copy-done.4
  1.5 0.0 copy-done.5
  1.5 0.0 copy-start
  1.5 1.2 %copy-done = bf16[64,7936]{1,0:T(8,128)(2,1)S(1)} copy-done((bf16[64,7936]{1,0:T(8,128)(2,1)S(1)}, bf16[64,7936]{1,0:T(8,128)(2,1)}, u32[]{:S(2)}) %copy-start) | copy-done | bytes 1015832
  2.7 0.0 copy-start.1
  2.7 0.9 copy-done.1
  3.6 0.0 copy-start.2
  3.6 0.9 copy-done.2
  4.5 0.0 copy-start.3
  4.5 0.9 copy-done.3
  5.4 99.4 %splade_head.1 = (f32[8,128]{1,0:T(8,128)S(1)}, f32[8,7936]{1,0:T(8,128)S(1)}, f32[3,7936]{1,0:T(4,128)S(1)}) custom-call(s32[3]{0:T(128)S(1)} %copy-done.4, bf16[64,768]{1,0:T(8,128)(2,1)S(1)} %bitcast.3, bf16[64,1024]{1,0:T(8,128)(2,1)S(1)} %copy-done.1, bf16[64,7936]{1,0:T(8,128)(2,1)S(1)} %copy-done, bf16[8,7936]{1,0:T(8,128)(2,1)S(1)} %copy-done.2, ...), custom_call_target="tpu_custom_call" | custom-call | tf_op jit(solution)/shard_map/splade_head/pallas_call | solution.py:545
  104.8 0.5 slice.3
  105.3 0.7 copy.12
  106.0 0.6 copy.13
Async XLA Ops:
  0.6 0.8 copy-start.4
  0.6 0.8 copy-start.5
  1.5 1.2 %copy-start = (bf16[64,7936]{1,0:T(8,128)(2,1)S(1)}, bf16[64,7936]{1,0:T(8,128)(2,1)}, u32[]{:S(2)}) copy-start(bf16[64,7936]{1,0:T(8,128)(2,1)} %weight.1) | copy-start | bytes 3047428
  2.7 0.9 copy-start.1
  3.6 0.9 copy-start.2
  4.5 0.9 copy-start.3

commit v3 on v2

--- a/solution.py
+++ b/solution.py
@@ -580,7 +580,7 @@
         + dma(7, 24, 32, 8, 8, 24, 32, 7, 16, 8, 3, 4)
         + dma(7, 16, 8, 2, 2, 3, 4, 3, 4, 7, 8),
         compiler_params=pltpu.CompilerParams(
-            collective_id=0, has_side_effects=True, vmem_limit_bytes=48 << 20
+            collective_id=0, has_side_effects=True, vmem_limit_bytes=58 << 20
         ),
         name="splade_head",
     )(lens, hid, dense, weight, queries, bias, positives)

time: 107 us -> 106 us (level)
  local copies, waits for them, and re-layouts: 6.56 us -> 4.93 us
    unnamed x14 -> x4, local copies, waits for them, and re-layouts: 5.26 us -> 2.35 us
where the time goes in v3:
time: 106 us
  Pallas kernels  100 us (94%)
  local copies, waits for them, and re-layouts  4.93 us (5%)
    pallas_call x1, Pallas kernels, call(): pl.pallas_call(kernel, out_shape=(jax.ShapeDtypeStruct((8, NQ), F32), jax...  100 us
    unnamed x4, local copies, waits for them, and re-layouts  2.35 us

profile of v3, /device:TPU:1, one launch (start us, length us, event | category | flops | bytes accessed | tf_op | source)
XLA Modules:
  0.0 105.7 jit_solution(5136255447951483868)
XLA Ops:
  0.6 1.4 %reshape.12.bias = f32[1,7936]{1,0:T(1,128)} reshape(f32[7936]{0:T(1024)} %param.10) | data formatting | bytes 63488 | tf_op jit(solution)/shard_map/reshape | solution.py:592
  2.0 100.1 %splade_head.1 = (f32[8,128]{1,0:T(8,128)}, f32[8,7936]{1,0:T(8,128)}, f32[3,7936]{1,0:T(4,128)}) custom-call(s32[3]{0:T(128)} %lens.1, bf16[64,768]{1,0:T(8,128)(2,1)} %bitcast.3, bf16[64,1024]{1,0:T(8,128)(2,1)} %dense.1, bf16[64,7936]{1,0:T(8,128)(2,1)} %weight.1, bf16[8,7936]{1,0:T(8,128)(2,1)} %queries.1, f32[1,7936]{1,0:T(1,128)} %reshape.12.bias, ...), custom_call_target="tpu_custom_call" | custom-call | tf_op jit(solution)/shard_map/splade_head/pallas_call | solution.py:545
  102.1 1.2 %slice.3 = f32[1,1]{1,0:T(1,128)} slice(f32[8,128]{1,0:T(8,128)} %get-tuple-element.6), slice={[0:1], [0:1]} | slice | bytes 8 | tf_op jit(solution)/shard_map/slice | solution.py:594
  103.3 0.0 copy-start
  103.3 1.7 %copy.12 = f32[8,7936]{1,0:T(8,128)} copy(f32[8,7936]{1,0:T(8,128)} %get-tuple-element.13) | data formatting | bytes 507904
  105.0 0.0 copy-done
  105.0 0.7 copy.13
Async XLA Ops:
  103.3 1.7 %copy-start = (f32[3,7936]{1,0:T(4,128)S(1)}, f32[3,7936]{1,0:T(4,128)}, u32[]{:S(2)}) copy-start(f32[3,7936]{1,0:T(4,128)} %get-tuple-element.14) | copy-start | bytes 285700
